TPU v7x, 128 devices: a whole 4x4x4 slice. The times are simulated.
128 devices in a mesh: row: 32 (over z, y, core), col: 4 (over x).
Axes of the slice: x: 4, y: 4, z: 4, core: 2. Of those that a mesh axis runs over, the one named last changes fastest.
Arguments:
- tokens: bfloat16 [16384, 2048], P('row', 'col'), may hold values from -6 to 6
- cotangent: bfloat16 [16384, 2048], P('row', 'col'), may hold values from -6 to 6
- destination: int32 [16384], P('row'), may hold values from 0 to 16383, as said below
- segment_ids: int32 [16384], P('row'), may hold values from 0 to 7, as said below
- attn_gain: float32 [2048], replicated, may hold values from 0.5 to 1.5
- w_query: bfloat16 [2048, 2048], P('row', 'col'), may hold values from -0.125 to 0.125
- w_key: bfloat16 [2048, 256], P('row', 'col'), may hold values from -0.125 to 0.125
- w_value: bfloat16 [2048, 256], P('row', 'col'), may hold values from -0.125 to 0.125
- w_output: bfloat16 [2048, 2048], P('row', 'col'), may hold values from -0.5 to 0.5
- ffn_gain: float32 [2048], replicated, may hold values from 0.5 to 1.5
- w_gate: bfloat16 [2048, 5632], P('row', 'col'), may hold values from -0.125 to 0.125
- w_up: bfloat16 [2048, 5632], P('row', 'col'), may hold values from -0.125 to 0.125
- w_down: bfloat16 [2048, 5632], P('row', 'col'), may hold values from -0.078125 to 0.078125
Outputs:
- output: bfloat16 [16384, 2048], P('row', 'col')
- input_grad: bfloat16 [16384, 2048], P('row', 'col')
- attn_gain_grad: float32 [2048], P('row')
- w_query_grad: float32 [2048, 2048], P('row', 'col')
- w_key_grad: float32 [2048, 256], P('row', 'col')
- w_value_grad: float32 [2048, 256], P('row', 'col')
- w_output_grad: float32 [2048, 2048], P('row', 'col')
- ffn_gain_grad: float32 [2048], P('row')
- w_gate_grad: float32 [2048, 5632], P('row', 'col')
- w_up_grad: float32 [2048, 5632], P('row', 'col')
- w_down_grad: float32 [2048, 5632], P('row', 'col')
Inputs may be any that keep to these rules, and one draw needn't show every extreme that they name: `destination`: A permutation; the tokens of each aligned block of 512 arriving tokens go to exactly 16 places in each aligned block of 512 balanced places. `segment_ids`: within each aligned block of 512 places the ids start at 0 and rise by one where a new sequence begins, so a block holds at most 8 sequences; in every draw some block holds a single sequence of 512 tokens and some block holds 8 sequences.
All inputs are finite; a program needn't handle non-finite values.
Results may differ from a plain program's by a relative error of at most 0.028.
Values may be sent and summed in bfloat16 or wider, within the bound.
No kernel may reach another device: no remote copies, remote signals or barrier semaphores. Data moves between devices by JAX's collectives and lax.ppermute only.
A program may use at most 128 MiB of HBM per device.

v0:
```python
from functools import partial
import jax
import jax.numpy as jnp
from jax import lax
from jax.sharding import PartitionSpec as P

HEADS = 32
KV = 4
HD = 64
EPS = 1e-05
ROPE_BASE = 10000.0


def rope_tables(positions):
    half_width = HD // 2
    freqs = ROPE_BASE ** (-(jnp.arange(half_width, dtype=jnp.float32) * 2.0 / HD))
    angles = positions.astype(jnp.float32)[:, None] * freqs[None, :]
    return (jnp.cos(angles)[:, None, :], jnp.sin(angles)[:, None, :])


def rotate(values, cosine, sine):
    half_width = values.shape[-1] // 2
    first = values[..., :half_width]
    second = values[..., half_width:]
    return jnp.concatenate(
        [first * cosine - second * sine, second * cosine + first * sine], axis=-1
    )


def rotate_back(grads, cosine, sine):
    half_width = grads.shape[-1] // 2
    first = grads[..., :half_width]
    second = grads[..., half_width:]
    return jnp.concatenate(
        [first * cosine + second * sine, second * cosine - first * sine], axis=-1
    )


def positions_of(segment_ids):
    index = jnp.arange(segment_ids.shape[0], dtype=jnp.int32)
    change = jnp.concatenate([jnp.ones((1,), dtype=jnp.bool_), segment_ids[1:] != segment_ids[:-1]])
    starts = jnp.where(change, index, jnp.zeros_like(index))
    return index - lax.cummax(starts, axis=0)


def allowed_pairs(segment_ids):
    index = jnp.arange(segment_ids.shape[0], dtype=jnp.int32)
    return (segment_ids[:, None] == segment_ids[None, :]) & (index[None, :] <= index[:, None])


def rms_scale(values):
    return lax.rsqrt(jnp.mean(values * values, axis=-1, keepdims=True) + EPS)


def norm_back(values, inv_root, gain, grads):
    normed = values * inv_root
    scaled = grads * gain
    result = inv_root * (scaled - normed * jnp.mean(scaled * normed, axis=-1, keepdims=True))
    return (result, jnp.sum(grads * normed, axis=0))


def matmul(left, right):
    return jnp.dot(left, right, preferred_element_type=jnp.float32)


def head_scores(query_head, key_head, allowed, scale_factor):
    scores = matmul(query_head, key_head.T) * scale_factor
    return jnp.where(allowed, scores, -1e30)


def head_forward(inputs, key_heads, value_heads, allowed, scale_factor):
    query_head, kv_slot = inputs
    scores = head_scores(query_head, key_heads[kv_slot], allowed, scale_factor)
    peak = jnp.max(scores, axis=-1, keepdims=True)
    expo = jnp.exp(scores - peak)
    total = jnp.sum(expo, axis=-1, keepdims=True)
    probs = expo / total
    mixed = matmul(probs.astype(jnp.bfloat16), value_heads[kv_slot])
    return (mixed, (peak + jnp.log(total))[:, 0])


def head_backward(inputs, key_heads, value_heads, allowed, scale_factor):
    query_head, kv_slot, grad_head, log_total = inputs
    key_head = key_heads[kv_slot]
    value_head = value_heads[kv_slot]
    scores = head_scores(query_head, key_head, allowed, scale_factor)
    probs = jnp.exp(scores - log_total[:, None])
    prob_grad = matmul(grad_head, value_head.T)
    value_grad = matmul(probs.astype(jnp.bfloat16).T, grad_head)
    inner = jnp.sum(probs * prob_grad, axis=-1, keepdims=True)
    score_grad = (probs * (prob_grad - inner)).astype(jnp.bfloat16)
    query_grad = matmul(score_grad, key_head) * scale_factor
    key_grad = matmul(score_grad.T, query_head) * scale_factor
    return (query_grad, key_grad, value_grad)


def body(
    tokens,
    cotangent,
    destination,
    segment_ids,
    attn_gain,
    w_query,
    w_key,
    w_value,
    w_output,
    ffn_gain,
    w_gate,
    w_up,
    w_down,
):
    row_count = tokens.shape[0]
    quarter = tokens.shape[1]
    col_start = lax.axis_index("col") * quarter
    group_size = HEADS // KV
    send_order = jnp.argsort(destination)
    slot_ids = destination[send_order] % row_count
    arrived_rows, arrived_grads, arrived_slots = (
        lax.all_to_all(tokens[send_order], "row", split_axis=0, concat_axis=0, tiled=True),
        lax.all_to_all(cotangent[send_order], "row", split_axis=0, concat_axis=0, tiled=True),
        lax.all_to_all(slot_ids, "row", split_axis=0, concat_axis=0, tiled=True),
    )
    placing = jnp.argsort(arrived_slots)
    full_rows, full_grads = (
        lax.all_gather(arrived_rows[placing], "col", axis=1, tiled=True),
        lax.all_gather(arrived_grads[placing], "col", axis=1, tiled=True),
    )
    query_w, key_w, value_w, output_w = (
        lax.all_gather(w_query, "row", axis=0, tiled=True),
        lax.all_gather(w_key, "row", axis=0, tiled=True),
        lax.all_gather(w_value, "row", axis=0, tiled=True),
        lax.all_gather(w_output, "row", axis=0, tiled=True),
    )
    cosine, sine = rope_tables(positions_of(segment_ids))
    allowed = allowed_pairs(segment_ids)
    rows_wide = full_rows.astype(jnp.float32)
    inv_one = rms_scale(rows_wide)
    normed_one = (rows_wide * inv_one * attn_gain).astype(jnp.bfloat16)
    query = matmul(normed_one, query_w)
    key_raw = matmul(normed_one, key_w)
    value_raw = matmul(normed_one, value_w)
    query_heads_count = query.shape[1] // HD
    kv_count = key_raw.shape[1] // HD
    query_rot = (
        rotate(query.reshape(row_count, query_heads_count, HD), cosine, sine)
        .astype(jnp.bfloat16)
        .transpose(1, 0, 2)
    )
    key_rot = (
        rotate(key_raw.reshape(row_count, kv_count, HD), cosine, sine)
        .astype(jnp.bfloat16)
        .transpose(1, 0, 2)
    )
    value_heads = value_raw.astype(jnp.bfloat16).reshape(row_count, kv_count, HD).transpose(1, 0, 2)
    kv_slots = jnp.arange(query_heads_count, dtype=jnp.int32) // group_size
    scale_factor = HD ** (-0.5)
    mixed_heads, log_totals = lax.map(
        partial(
            head_forward,
            key_heads=key_rot,
            value_heads=value_heads,
            allowed=allowed,
            scale_factor=scale_factor,
        ),
        (query_rot, kv_slots),
    )
    mixed = (
        mixed_heads.transpose(1, 0, 2)
        .reshape(row_count, query_heads_count * HD)
        .astype(jnp.bfloat16)
    )
    attn_terms = matmul(mixed, output_w.T)
    attn_full = lax.psum(attn_terms, "col")
    resid = rows_wide + attn_full
    inv_two = rms_scale(resid)
    normed_two = (resid * inv_two * ffn_gain).astype(jnp.bfloat16)
    resid_part = lax.dynamic_slice_in_dim(resid, col_start, quarter, 1)
    gate_w, up_w, down_w = (
        lax.all_gather(w_gate, "row", axis=0, tiled=True),
        lax.all_gather(w_up, "row", axis=0, tiled=True),
        lax.all_gather(w_down, "row", axis=0, tiled=True),
    )
    gate = matmul(normed_two, gate_w)
    upper = matmul(normed_two, up_w)
    sigmoid_gate = jax.nn.sigmoid(gate)
    activ = (gate * sigmoid_gate * upper).astype(jnp.bfloat16)
    ffn_share = lax.psum_scatter(
        matmul(activ, down_w.T).astype(jnp.bfloat16), "col", scatter_dimension=1, tiled=True
    ).astype(jnp.float32)
    output_share = (resid_part + ffn_share).astype(jnp.bfloat16)
    gate_w, up_w, down_w = (
        lax.all_gather(w_gate, "row", axis=0, tiled=True),
        lax.all_gather(w_up, "row", axis=0, tiled=True),
        lax.all_gather(w_down, "row", axis=0, tiled=True),
    )
    down_weight_grad = matmul(full_grads.T, activ)
    act_grad = matmul(full_grads, down_w)
    gate_grad = (act_grad * upper * sigmoid_gate * (1.0 + gate * (1.0 - sigmoid_gate))).astype(
        jnp.bfloat16
    )
    up_grad = (act_grad * gate * sigmoid_gate).astype(jnp.bfloat16)
    gate_weight_grad = matmul(normed_two.T, gate_grad)
    up_weight_grad = matmul(normed_two.T, up_grad)
    normed_terms_two = matmul(gate_grad, gate_w.T) + matmul(up_grad, up_w.T)
    normed_grad_two = lax.psum(normed_terms_two, "col")
    resid_norm_grad, ffn_gain_grad = norm_back(resid, inv_two, ffn_gain, normed_grad_two)
    resid_grad = full_grads.astype(jnp.float32) + resid_norm_grad
    attn_grad_low = resid_grad.astype(jnp.bfloat16)
    ffn_results = (
        lax.psum_scatter(
            gate_weight_grad.astype(jnp.bfloat16), "row", scatter_dimension=0, tiled=True
        ).astype(jnp.float32),
        lax.psum_scatter(
            up_weight_grad.astype(jnp.bfloat16), "row", scatter_dimension=0, tiled=True
        ).astype(jnp.float32),
        lax.psum_scatter(
            down_weight_grad.astype(jnp.bfloat16), "row", scatter_dimension=0, tiled=True
        ).astype(jnp.float32),
        lax.psum_scatter(
            ffn_gain_grad.astype(jnp.bfloat16), "row", scatter_dimension=0, tiled=True
        ).astype(jnp.float32),
    )
    query_w, key_w, value_w, output_w = (
        lax.all_gather(w_query, "row", axis=0, tiled=True),
        lax.all_gather(w_key, "row", axis=0, tiled=True),
        lax.all_gather(w_value, "row", axis=0, tiled=True),
        lax.all_gather(w_output, "row", axis=0, tiled=True),
    )
    output_weight_grad = matmul(attn_grad_low.T, mixed)
    mixed_grad = matmul(attn_grad_low, output_w).astype(jnp.bfloat16)
    mixed_grad_heads = mixed_grad.reshape(row_count, query_heads_count, HD).transpose(1, 0, 2)
    query_grads, key_grads, value_grads = lax.map(
        partial(
            head_backward,
            key_heads=key_rot,
            value_heads=value_heads,
            allowed=allowed,
            scale_factor=scale_factor,
        ),
        (query_rot, kv_slots, mixed_grad_heads, log_totals),
    )
    query_grad = (
        rotate_back(query_grads.transpose(1, 0, 2), cosine, sine)
        .reshape(row_count, query_heads_count * HD)
        .astype(jnp.bfloat16)
    )
    key_sum = key_grads.reshape(kv_count, group_size, row_count, HD).sum(axis=1).transpose(1, 0, 2)
    key_grad = (
        rotate_back(key_sum, cosine, sine).reshape(row_count, kv_count * HD).astype(jnp.bfloat16)
    )
    value_sum = (
        value_grads.reshape(kv_count, group_size, row_count, HD).sum(axis=1).transpose(1, 0, 2)
    )
    value_grad = value_sum.reshape(row_count, kv_count * HD).astype(jnp.bfloat16)
    query_weight_grad = matmul(normed_one.T, query_grad)
    key_weight_grad = matmul(normed_one.T, key_grad)
    value_weight_grad = matmul(normed_one.T, value_grad)
    normed_terms_one = (
        matmul(query_grad, query_w.T) + matmul(key_grad, key_w.T) + matmul(value_grad, value_w.T)
    )
    normed_grad_one = lax.psum(normed_terms_one.astype(jnp.bfloat16), "col").astype(jnp.float32)
    rows_norm_grad, attn_gain_grad = norm_back(rows_wide, inv_one, attn_gain, normed_grad_one)
    rows_grad = resid_grad + rows_norm_grad
    input_share = lax.dynamic_slice_in_dim(rows_grad, col_start, quarter, 1).astype(jnp.bfloat16)
    attn_results = (
        lax.psum_scatter(
            query_weight_grad.astype(jnp.bfloat16), "row", scatter_dimension=0, tiled=True
        ).astype(jnp.float32),
        lax.psum_scatter(
            key_weight_grad.astype(jnp.bfloat16), "row", scatter_dimension=0, tiled=True
        ).astype(jnp.float32),
        lax.psum_scatter(
            value_weight_grad.astype(jnp.bfloat16), "row", scatter_dimension=0, tiled=True
        ).astype(jnp.float32),
        lax.psum_scatter(
            output_weight_grad.astype(jnp.bfloat16), "row", scatter_dimension=0, tiled=True
        ).astype(jnp.float32),
        lax.psum_scatter(
            attn_gain_grad.astype(jnp.bfloat16), "row", scatter_dimension=0, tiled=True
        ).astype(jnp.float32),
    )
    back_rows, back_grads = (
        lax.all_to_all(output_share[arrived_slots], "row", split_axis=0, concat_axis=0, tiled=True),
        lax.all_to_all(input_share[arrived_slots], "row", split_axis=0, concat_axis=0, tiled=True),
    )
    restore = jnp.argsort(send_order)
    return (
        back_rows[restore],
        back_grads[restore],
        attn_results[4],
        attn_results[0],
        attn_results[1],
        attn_results[2],
        attn_results[3],
        ffn_results[3],
        ffn_results[0],
        ffn_results[1],
        ffn_results[2],
    )


def solution(mesh):
    placed = (
        P("row", "col"),
        P("row", "col"),
        P("row"),
        P("row"),
        P(),
        P("row", "col"),
        P("row", "col"),
        P("row", "col"),
        P("row", "col"),
        P(),
        P("row", "col"),
        P("row", "col"),
        P("row", "col"),
    )
    return jax.shard_map(
        body,
        mesh=mesh,
        in_specs=placed,
        out_specs=(
            P("row", "col"),
            P("row", "col"),
            P("row"),
            P("row", "col"),
            P("row", "col"),
            P("row", "col"),
            P("row", "col"),
            P("row"),
            P("row", "col"),
            P("row", "col"),
            P("row", "col"),
        ),
        check_vma=False,
    )
```

profile of v0, /device:TPU:0, one launch (start us, length us, event | category | flops | bytes accessed | tf_op | source)
XLA Modules:
  0.0 1312.7 jit_solution(15525933860058886407)
XLA Ops:
  16.6 8.4 all-to-all-start.1
  53.0 22.4 %all_gather.36 = bf16[2048,64]{1,0:T(8,128)(2,1)S(1)} all-gather(bf16[64,64]{1,0:T(8,128)(2,1)S(1)} %copy-done.22), channel_id=1, replica_groups=mesh['row'=32,'col'=4] {'row'}, dimensions={0}, use_global_device_ids=true | all-gather | bytes 270336 | tf_op jit(solution)/shard_map/all_gather | solution.py:130
  75.5 26.7 %all_gather.37 = bf16[2048,64]{1,0:T(8,128)(2,1)} all-gather(bf16[64,64]{1,0:T(8,128)(2,1)S(1)} %copy-done.23), channel_id=1, replica_groups=mesh['row'=32,'col'=4] {'row'}, dimensions={0}, use_global_device_ids=true | all-gather | bytes 270336 | tf_op jit(solution)/shard_map/all_gather | solution.py:131
  111.2 14.4 %all-gather.10.cloned.1.call-done = bf16[2048,512]{1,0:T(8,128)(2,1)} async-done(((bf16[64,512]{1,0:T(8,128)(2,1)}), bf16[2048,512]{1,0:T(8,128)(2,1)}) %all-gather.10.cloned.1.call-update) | async-done | bytes 2097168 | tf_op jit(solution)/shard_map/all_gather | solution.py:129
  129.4 24.0 %while.32 = (s32[]{:T(128)}, bf16[8,512,64]{1,2,0:T(8,128)(2,1)S(1)}, f32[8,512]{1,0:T(8,128)}, bf16[8,512,64]{2,1,0:T(8,128)(2,1)S(1)}, bf16[1,512,64]{2,1,0:T(...) while((s32[]{:T(128)}, bf16[8,512,64]{1,2,0:T(8,128)(2,1)S(1)}, ...), condition=%wide.region_8.9_spmd.clone.clone, body=%wide.region_5.8_spmd.clone.sunk.clone | while | flops 69991936 | bytes 3695189 | solution.py:157
  153.4 17.8 %all-gather.12.cloned.1.call-done = bf16[2048,512]{1,0:T(8,128)(2,1)} async-done(((bf16[64,512]{1,0:T(8,128)(2,1)}), bf16[2048,512]{1,0:T(8,128)(2,1)}) %all-gather.12.cloned.1.call-update) | async-done | bytes 2097168 | tf_op jit(solution)/shard_map/all_gather | solution.py:132
  180.0 17.1 %all_to_all.60 = bf16[32,16,512]{2,1,0:T(8,128)(2,1)S(1)} all-to-all(bf16[32,16,512]{2,1,0:T(8,128)(2,1)} %bitcast.194), channel_id=1, replica_groups=mesh['row'=32,'col'=4] {'row'}, dimensions={0} | all-to-all | bytes 1048576 | tf_op jit(solution)/shard_map/all_to_all | solution.py:120
  201.1 67.2 %all-reduce.7.cloned.1.call-done = f32[512,2048]{1,0:T(8,128)} async-done(((f32[512,2048]{1,0:T(8,128)}), f32[512,2048]{1,0:T(8,128)}) %all-reduce.7.cloned.1.call-update) | async-done | bytes 4194320 | tf_op jit(solution)/shard_map/psum | solution.py:173
  274.8 44.2 %all-gather.14.cloned.1.call-done = bf16[2048,1408]{1,0:T(8,128)(2,1)} async-done(((bf16[64,1408]{1,0:T(8,128)(2,1)}), bf16[2048,1408]{1,0:T(8,128)(2,1)}) %all-gather.14.cloned.1.call-update) | async-done | bytes 5767184 | tf_op jit(solution)/shard_map/all_gather | solution.py:179
  319.0 8.3 fusion.76
  327.3 41.5 %all-gather.16.cloned.1.call-done = bf16[2048,1408]{1,0:T(8,128)(2,1)} async-done(((bf16[64,1408]{1,0:T(8,128)(2,1)}), bf16[2048,1408]{1,0:T(8,128)(2,1)}) %all-gather.16.cloned.1.call-update) | async-done | bytes 5767184 | tf_op jit(solution)/shard_map/all_gather | solution.py:180
  368.8 8.3 fusion.77
  377.1 23.9 %all-gather.22.cloned.1.call-done = bf16[512,2048]{1,0:T(8,128)(2,1)} async-done(((bf16[512,512]{1,0:T(8,128)(2,1)}), bf16[512,2048]{1,0:T(8,128)(2,1)}) %all-gather.22.cloned.1.call-update) | async-done | bytes 2097168 | tf_op jit(solution)/shard_map/all_gather | solution.py:126
  400.9 51.0 %all-gather.18.cloned.1.call-done = bf16[2048,1408]{1,0:T(8,128)(2,1)} async-done(((bf16[64,1408]{1,0:T(8,128)(2,1)}), bf16[2048,1408]{1,0:T(8,128)(2,1)}) %all-gather.18.cloned.1.call-update) | async-done | bytes 5767184 | tf_op jit(solution)/shard_map/all_gather | solution.py:181
  452.0 10.3 multiply_convert_fusion.3
  474.2 7.9 convolution_convert_fusion.5
  482.2 83.7 %all-reduce.9.cloned.1.call-done = f32[512,2048]{1,0:T(8,128)} async-done(((f32[512,2048]{1,0:T(8,128)}), f32[512,2048]{1,0:T(8,128)}) %all-reduce.9.cloned.1.call-update) | async-done | bytes 4194320 | tf_op jit(solution)/shard_map/psum | solution.py:205
  579.3 65.5 %while.33 = (s32[]{:T(128)}, f32[8,512,64]{1,2,0:T(8,128)}, f32[8,512,64]{1,2,0:T(8,128)}, f32[8,512,64]{1,2,0:T(8,128)}, bf16[8,512,64]{2,1,0:T(8,128)(2,1)}, /...) while((s32[]{:T(128)}, f32[8,512,64]{1,2,0:T(8,128)}, ...), condition=%wide.region_17.18_spmd.clone.clone, body=%wide.region_15.17_spmd.clone.sunk.clone | while | flops 170982912 | bytes 8996457 | solution.py:232
  667.5 8.0 convolution_convert_fusion.2
  675.5 8.1 convolution_convert_fusion.1
  683.9 7.9 convolution_convert_fusion
  696.3 7.3 all-to-all-start.2
  703.5 10.4 all-reduce.11.cloned.1.call-done
  721.0 7.3 all-to-all-start.4
  733.4 61.5 %reduce-scatter.13.cloned.1.call-done = bf16[64,64]{1,0:T(8,128)(2,1)} async-done(((bf16[2048,64]{1,0:T(8,128)(2,1)}), bf16[64,64]{1,0:T(8,128)(2,1)}) %reduce-scatter.13.cloned.1.call-update) | async-done | bytes 8208 | tf_op jit(solution)/shard_map/reduce_scatter | solution.py:269
  796.2 78.5 %reduce-scatter.15.cloned.1.call-done = bf16[64,64]{1,0:T(8,128)(2,1)} async-done(((bf16[2048,64]{1,0:T(8,128)(2,1)}), bf16[64,64]{1,0:T(8,128)(2,1)}) %reduce-scatter.15.cloned.1.call-update) | async-done | bytes 8208 | tf_op jit(solution)/shard_map/reduce_scatter | solution.py:272
  878.7 64.4 %all-reduce.2 = (bf16[2048]{0:T(1024)(128)(2,1)S(1)}, bf16[2048]{0:T(1024)(128)(2,1)S(1)}) all-reduce(bf16[2048]{0:T(1024)(128)(2,1)S(1)} %get-tuple-element.249, bf16[2048]{0:T(1024)(128)(2,1)S(1)} %copy-done.20), channel_id=5, replica_groups=mesh['row'=32,'col'=4] {'row'}, use_global_device_ids=true, to_apply=%region_23.24.clone | all-reduce | flops 4096 | bytes 16384
  946.4 10.0 reduce-scatter.11.cloned.1.call-done
  957.9 80.2 %reduce-scatter.17.cloned.1.call-done = bf16[64,512]{1,0:T(8,128)(2,1)} async-done(((bf16[2048,512]{1,0:T(8,128)(2,1)}), bf16[64,512]{1,0:T(8,128)(2,1)}) %reduce-scatter.17.cloned.1.call-update) | async-done | bytes 65552 | tf_op jit(solution)/shard_map/reduce_scatter | solution.py:275
  1039.6 86.9 %reduce-scatter.19.cloned.1.call-done = bf16[64,1408]{1,0:T(8,128)(2,1)} async-done(((bf16[2048,1408]{1,0:T(8,128)(2,1)}), bf16[64,1408]{1,0:T(8,128)(2,1)}) %reduce-scatter.19.cloned.1.call-update) | async-done | bytes 180240 | tf_op jit(solution)/shard_map/reduce_scatter | solution.py:210
  1128.2 87.2 %reduce-scatter.21.cloned.1.call-done = bf16[64,1408]{1,0:T(8,128)(2,1)} async-done(((bf16[2048,1408]{1,0:T(8,128)(2,1)}), bf16[64,1408]{1,0:T(8,128)(2,1)}) %reduce-scatter.21.cloned.1.call-update) | async-done | bytes 180240 | tf_op jit(solution)/shard_map/reduce_scatter | solution.py:213
  1217.0 86.7 %reduce-scatter.23.cloned.1.call-done = bf16[64,1408]{1,0:T(8,128)(2,1)} async-done(((bf16[2048,1408]{1,0:T(8,128)(2,1)}), bf16[64,1408]{1,0:T(8,128)(2,1)}) %reduce-scatter.23.cloned.1.call-update) | async-done | bytes 180240 | tf_op jit(solution)/shard_map/reduce_scatter | solution.py:216
  (298 shorter events, 239.0 us)
Async XLA Ops:
  16.6 15.7 %all-to-all-start.1 = ((s32[32,16,1]{1,2,0:T(1,128)}), s32[32,16,1]{1,2,0:T(1,128)S(1)}, u32[]{:S(2)}, u32[]{:S(2)}) async-start(s32[32,16,1]{1,2,0:T(1,128)} %bitcast.2), calls=%async_computation.1 | async-start | bytes 32768 | tf_op jit(solution)/shard_map/all_to_all | solution.py:121
  27.7 25.3 %copy-start.22 = (bf16[64,64]{1,0:T(8,128)(2,1)S(1)}, bf16[64,64]{1,0:T(8,128)(2,1)}, u32[]{:S(2)}) copy-start(bf16[64,64]{1,0:T(8,128)(2,1)} %param.23) | copy-start | bytes 24580
  27.7 47.8 %copy-start.23 = (bf16[64,64]{1,0:T(8,128)(2,1)S(1)}, bf16[64,64]{1,0:T(8,128)(2,1)}, u32[]{:S(2)}) copy-start(bf16[64,64]{1,0:T(8,128)(2,1)} %param.24) | copy-start | bytes 24580
  32.3 15.7 %all-to-all-start = ((bf16[32,16,512]{2,1,0:T(8,128)(2,1)}), bf16[32,16,512]{2,1,0:T(8,128)(2,1)S(1)}, u32[]{:S(2)}, u32[]{:S(2)}) async-start(bf16[32,16,512]{2,1,0:T(8,128)(2,1)} %bitcast), calls=%async_computation | async-start | bytes 1048576 | tf_op jit(solution)/shard_map/all_to_all | solution.py:119
  36.2 66.3 %all-gather.20.cloned.1.call-start = ((), (), s32[]{:S(2)}) async-start(), calls=%async_computation.29 | async-start | bytes 2621440 | tf_op jit(solution)/shard_map/all_gather | solution.py:125
  48.0 56.8 %copy-start.24 = (f32[2048]{0:T(1024)S(1)}, f32[2048]{0:T(1024)}, u32[]{:S(2)}) copy-start(f32[2048]{0:T(1024)} %param.21) | copy-start | bytes 24580
  50.6 75.0 %all-gather.10.cloned.1.call-start = ((), (), s32[]{:S(2)}) async-start(), calls=%async_computation.13 | async-start | bytes 2162688 | tf_op jit(solution)/shard_map/all_gather | solution.py:129
  51.4 119.8 %all-gather.12.cloned.1.call-start = ((), (), s32[]{:S(2)}) async-start(), calls=%async_computation.14 | async-start | bytes 2162688 | tf_op jit(solution)/shard_map/all_gather | solution.py:132
  52.1 216.2 %all-reduce.7.cloned.1.call-start = ((), (), s32[]{:S(2)}) async-start(), calls=%async_computation.15 | async-start | bytes 8388608 | tf_op jit(solution)/shard_map/psum | solution.py:173
  52.2 55.4 %copy-start.29 = (f32[32]{0:T(128)}, f32[32]{0:T(128)S(1)}, u32[]{:S(2)}) copy-start(f32[32]{0:T(128)S(1)} %negate_power_fusion) | copy-start | bytes 388
  53.0 54.5 %copy-start.15 = (f32[512]{0:T(512)}, f32[512]{0:T(512)S(1)}, u32[]{:S(2)}) copy-start(f32[512]{0:T(512)S(1)} %fusion.70) | copy-start | bytes 6148
  75.5 34.8 %copy-start.10 = (bf16[2048,64]{1,0:T(8,128)(2,1)}, bf16[2048,64]{1,0:T(8,128)(2,1)S(1)}, u32[]{:S(2)}) copy-start(bf16[2048,64]{1,0:T(8,128)(2,1)S(1)} %all_gather.36) | copy-start | bytes 786436
  176.1 142.8 %all-gather.14.cloned.1.call-start = ((), (), s32[]{:S(2)}) async-start(), calls=%async_computation.16 | async-start | bytes 5947392 | tf_op jit(solution)/shard_map/all_gather | solution.py:179
  176.7 192.1 %all-gather.16.cloned.1.call-start = ((), (), s32[]{:S(2)}) async-start(), calls=%async_computation.17 | async-start | bytes 5947392 | tf_op jit(solution)/shard_map/all_gather | solution.py:180
  177.3 223.6 %all-gather.22.cloned.1.call-start = ((), (), s32[]{:S(2)}) async-start(), calls=%async_computation.30 | async-start | bytes 2621440 | tf_op jit(solution)/shard_map/all_gather | solution.py:126
  180.0 88.3 %copy-start.7 = (bf16[512,2048]{1,0:T(8,128)(2,1)S(1)}, bf16[512,2048]{1,0:T(8,128)(2,1)}, u32[]{:S(2)}) copy-start(bf16[512,2048]{1,0:T(8,128)(2,1)} %all-gather.20.cloned.1.call-done) | copy-start | bytes 6291460
  199.9 252.1 %all-gather.18.cloned.1.call-start = ((), (), s32[]{:S(2)}) async-start(), calls=%async_computation.18 | async-start | bytes 5947392 | tf_op jit(solution)/shard_map/all_gather | solution.py:181
  200.6 72.4 %copy-start.14 = (f32[2048]{0:T(1024)S(1)}, f32[2048]{0:T(1024)}, u32[]{:S(2)}) copy-start(f32[2048]{0:T(1024)} %param.26) | copy-start | bytes 24580
  200.6 365.2 %all-reduce.9.cloned.1.call-start = ((), (), s32[]{:S(2)}) async-start(), calls=%async_computation.20 | async-start | bytes 8388608 | tf_op jit(solution)/shard_map/psum | solution.py:205
  474.0 218.0 %reduce-scatter.9.cloned.1.call-start = ((), (), s32[]{:S(2)}) async-start(), calls=%async_computation.19 | async-start | bytes 2621440 | tf_op jit(solution)/shard_map/reduce_scatter | solution.py:187
  482.1 231.8 %all-reduce.11.cloned.1.call-start = ((), (), s32[]{:S(2)}) async-start(), calls=%async_computation.21 | async-start | bytes 4194304 | tf_op jit(solution)/shard_map/psum | solution.py:261
  655.2 139.7 %reduce-scatter.13.cloned.1.call-start = ((), (), s32[]{:S(2)}) async-start(), calls=%async_computation.23 | async-start | bytes 540672 | tf_op jit(solution)/shard_map/reduce_scatter | solution.py:269
  657.1 217.6 %reduce-scatter.15.cloned.1.call-start = ((), (), s32[]{:S(2)}) async-start(), calls=%async_computation.24 | async-start | bytes 540672 | tf_op jit(solution)/shard_map/reduce_scatter | solution.py:272
  659.2 297.1 %reduce-scatter.11.cloned.1.call-start = ((), (), s32[]{:S(2)}) async-start(), calls=%async_computation.22 | async-start | bytes 2162688 | tf_op jit(solution)/shard_map/reduce_scatter | solution.py:266
  662.1 375.9 %reduce-scatter.17.cloned.1.call-start = ((), (), s32[]{:S(2)}) async-start(), calls=%async_computation.25 | async-start | bytes 2162688 | tf_op jit(solution)/shard_map/reduce_scatter | solution.py:275
  667.4 459.0 %reduce-scatter.19.cloned.1.call-start = ((), (), s32[]{:S(2)}) async-start(), calls=%async_computation.26 | async-start | bytes 5947392 | tf_op jit(solution)/shard_map/reduce_scatter | solution.py:210
  675.5 539.8 %reduce-scatter.21.cloned.1.call-start = ((), (), s32[]{:S(2)}) async-start(), calls=%async_computation.27 | async-start | bytes 5947392 | tf_op jit(solution)/shard_map/reduce_scatter | solution.py:213
  683.6 620.1 %reduce-scatter.23.cloned.1.call-start = ((), (), s32[]{:S(2)}) async-start(), calls=%async_computation.28 | async-start | bytes 5947392 | tf_op jit(solution)/shard_map/reduce_scatter | solution.py:216
  696.3 24.8 %all-to-all-start.2 = ((bf16[32,16,512]{2,1,0:T(8,128)(2,1)}), bf16[32,16,512]{2,1,0:T(8,128)(2,1)S(1)}, u32[]{:S(2)}, u32[]{:S(2)}) async-start(bf16[32,16,512]{2,1,0:T(8,128)(2,1)} %bitcast.14), calls=%async_computation.3 | async-start | bytes 1048576 | tf_op jit(solution)/shard_map/all_to_all | solution.py:283
  718.4 160.3 %copy-start.20 = (bf16[2048]{0:T(1024)(128)(2,1)S(1)}, bf16[2048]{0:T(1024)(128)(2,1)}, u32[]{:S(2)}) copy-start(bf16[2048]{0:T(1024)(128)(2,1)} %get-tuple-element.247) | copy-start | bytes 12292
  721.0 222.7 %all-to-all-start.4 = ((bf16[32,16,512]{2,1,0:T(8,128)(2,1)}), bf16[32,16,512]{2,1,0:T(8,128)(2,1)S(1)}, u32[]{:S(2)}, u32[]{:S(2)}) async-start(bf16[32,16,512]{2,1,0:T(8,128)(2,1)} %bitcast.24), calls=%async_computation.5 | async-start | bytes 1048576 | tf_op jit(solution)/shard_map/all_to_all | solution.py:284
  876.1 429.3 %copy-start.1 = (bf16[512,512]{1,0:T(8,128)(2,1)S(1)}, bf16[512,512]{1,0:T(8,128)(2,1)}, u32[]{:S(2)}) copy-start(bf16[512,512]{1,0:T(8,128)(2,1)} %param.17) | copy-start | bytes 1572868
  (24 other events, 188.3 us)
Sparse Core Ops, SparseCore 0:
  50.7 28.4 all-gather.19
  81.5 44.0 all-gather.9
  127.9 43.2 all-gather.11
  176.2 91.9 all-reduce.6
  270.6 48.3 all-gather.13
  321.3 47.4 all-gather.15
  371.1 29.7 all-gather.21
  403.4 48.4 all-gather.17
  474.1 91.7 all-reduce.8
  568.1 29.5 reduce-scatter.8
  655.3 58.5 all-reduce.10
  717.8 77.0 reduce-scatter.12
  798.4 76.3 reduce-scatter.14
  878.2 78.1 reduce-scatter.10
  959.8 78.2 reduce-scatter.16
  1041.7 84.7 reduce-scatter.18
  1130.5 84.7 reduce-scatter.20
  1218.9 84.7 reduce-scatter.22
where the time goes:
time: 1320 us; the launch traced here: 1310 us
  waiting for transfers between devices  860 us (65%)
  matrix products  170 us (13%)
  blocking collectives  131 us (10%)
  other arithmetic  55.9 us (4%)
  local copies, waits for them, and re-layouts  51.2 us (4%)
  starting transfers between devices  28.6 us (2%)
  between operations  16 us (1%)
    dot_general x77, matrix products, matmul(): return jnp.dot(left, right, preferred_element_type=jnp.float32)  170 us
    reduce_scatter x1, waiting for transfers between devices, body(): lax.psum_scatter(up_weight_grad.astype(jnp.bfloat16), 'row', scatter_dime...  87.2 us
    reduce_scatter x1, waiting for transfers between devices, body(): lax.psum_scatter(gate_weight_grad.astype(jnp.bfloat16), 'row', scatter_di...  86.9 us
    reduce_scatter x1, waiting for transfers between devices, body(): lax.psum_scatter(down_weight_grad.astype(jnp.bfloat16), 'row', scatter_di...  86.7 us
    psum x1, waiting for transfers between devices, body(): normed_grad_two = lax.psum(normed_terms_two, 'col')  83.7 us
    reduce_scatter x1, waiting for transfers between devices, body(): lax.psum_scatter(output_weight_grad.astype(jnp.bfloat16), 'row', scatter_...  80.2 us
    reduce_scatter x1, waiting for transfers between devices, body(): lax.psum_scatter(value_weight_grad.astype(jnp.bfloat16), 'row', scatter_d...  78.5 us
    psum x1, waiting for transfers between devices, body(): attn_full = lax.psum(attn_terms, 'col')  67.2 us
  transfers between devices with their start and end apart: 22, of which 18 were waited for; matrix products, arithmetic and copies ran while one was open for 18% of the time, Pallas kernels for 0%

commit v1 on v0

--- a/solution.py
+++ b/solution.py
@@ -175,8 +175,16 @@
     inv_two = rms_scale(resid)
     normed_two = (resid * inv_two * ffn_gain).astype(jnp.bfloat16)
     resid_part = lax.dynamic_slice_in_dim(resid, col_start, quarter, 1)
+
+    def set_column_up(block_here):
+        taken_in = jnp.stack([block_here for _ in range(lax.axis_size("row"))])
+        u1 = jnp.concatenate(
+            lax.all_to_all(taken_in, split_axis=0, concat_axis=0, axis_name="row"), axis=0
+        )
+        return u1
+
     gate_w, up_w, down_w = (
-        lax.all_gather(w_gate, "row", axis=0, tiled=True),
+        set_column_up(w_gate),
         lax.all_gather(w_up, "row", axis=0, tiled=True),
         lax.all_gather(w_down, "row", axis=0, tiled=True),
     )

time: 1320 us -> 1310 us (level)
  waiting for transfers between devices: 860 us -> 837 us
  transfers between devices with their start and end apart: 22 -> 23, of which waited for: 18 -> 19; matrix products, arithmetic and copies ran while one was open for 18% -> 19% of each run, Pallas kernels for 0% -> 0%
where the time goes in v1:
time: 1310 us; the launch traced here: 1300 us
  waiting for transfers between devices  837 us (64%)
  matrix products  172 us (13%)
  blocking collectives  131 us (10%)
  local copies, waits for them, and re-layouts  56.6 us (4%)
  other arithmetic  55.9 us (4%)
  starting transfers between devices  33.5 us (3%)
  between operations  16 us (1%)
    dot_general x77, matrix products, matmul(): return jnp.dot(left, right, preferred_element_type=jnp.float32)  172 us
    reduce_scatter x1, waiting for transfers between devices, body(): lax.psum_scatter(up_weight_grad.astype(jnp.bfloat16), 'row', scatter_dime...  87.1 us
    reduce_scatter x1, waiting for transfers between devices, body(): lax.psum_scatter(gate_weight_grad.astype(jnp.bfloat16), 'row', scatter_di...  86.8 us
    reduce_scatter x1, waiting for transfers between devices, body(): lax.psum_scatter(down_weight_grad.astype(jnp.bfloat16), 'row', scatter_di...  86.6 us
    psum x1, waiting for transfers between devices, body(): normed_grad_two = lax.psum(normed_terms_two, 'col')  83.7 us
    reduce_scatter x1, waiting for transfers between devices, body(): lax.psum_scatter(output_weight_grad.astype(jnp.bfloat16), 'row', scatter_...  80.2 us
    reduce_scatter x1, waiting for transfers between devices, body(): lax.psum_scatter(value_weight_grad.astype(jnp.bfloat16), 'row', scatter_d...  78.5 us
    unnamed x1, blocking collectives  64.4 us
  transfers between devices with their start and end apart: 23, of which 19 were waited for; matrix products, arithmetic and copies ran while one was open for 19% of the time, Pallas kernels for 0%

profile of v1, /device:TPU:0, one launch (start us, length us, event | category | flops | bytes accessed | tf_op | source)
XLA Modules:
  0.0 1301.4 jit_solution(4121244902759686115)
XLA Ops:
  16.6 8.4 all-to-all-start.1
  53.0 22.4 %all_gather.35 = bf16[2048,64]{1,0:T(8,128)(2,1)S(1)} all-gather(bf16[64,64]{1,0:T(8,128)(2,1)S(1)} %copy-done.19), channel_id=1, replica_groups=mesh['row'=32,'col'=4] {'row'}, dimensions={0}, use_global_device_ids=true | all-gather | bytes 270336 | tf_op jit(solution)/shard_map/all_gather | solution.py:130
  75.5 26.7 %all_gather.36 = bf16[2048,64]{1,0:T(8,128)(2,1)} all-gather(bf16[64,64]{1,0:T(8,128)(2,1)S(1)} %copy-done.20), channel_id=1, replica_groups=mesh['row'=32,'col'=4] {'row'}, dimensions={0}, use_global_device_ids=true | all-gather | bytes 270336 | tf_op jit(solution)/shard_map/all_gather | solution.py:131
  111.3 14.4 %all-gather.10.cloned.1.call-done = bf16[2048,512]{1,0:T(8,128)(2,1)} async-done(((bf16[64,512]{1,0:T(8,128)(2,1)}), bf16[2048,512]{1,0:T(8,128)(2,1)}) %all-gather.10.cloned.1.call-update) | async-done | bytes 2097168 | tf_op jit(solution)/shard_map/all_gather | solution.py:129
  130.2 25.2 %while.32 = (s32[]{:T(128)}, bf16[8,512,64]{1,2,0:T(8,128)(2,1)S(1)}, f32[8,512]{1,0:T(8,128)}, bf16[8,512,64]{2,1,0:T(8,128)(2,1)}, bf16[1,512,64]{2,1,0:T(8,12...) while((s32[]{:T(128)}, bf16[8,512,64]{1,2,0:T(8,128)(2,1)S(1)}, ...), condition=%wide.region_8.9_spmd.clone.clone, body=%wide.region_5.8_spmd.clone.sunk.clone | while | flops 69991936 | bytes 3629153 | solution.py:157
  155.4 15.8 %all-gather.12.cloned.1.call-done = bf16[2048,512]{1,0:T(8,128)(2,1)} async-done(((bf16[64,512]{1,0:T(8,128)(2,1)}), bf16[2048,512]{1,0:T(8,128)(2,1)}) %all-gather.12.cloned.1.call-update) | async-done | bytes 2097168 | tf_op jit(solution)/shard_map/all_gather | solution.py:132
  179.8 17.0 %all_to_all.65 = bf16[32,16,512]{2,1,0:T(8,128)(2,1)S(1)} all-to-all(bf16[32,16,512]{2,1,0:T(8,128)(2,1)} %bitcast.196), channel_id=1, replica_groups=mesh['row'=32,'col'=4] {'row'}, dimensions={0} | all-to-all | bytes 1048576 | tf_op jit(solution)/shard_map/all_to_all | solution.py:120
  210.6 57.6 %all-reduce.7.cloned.1.call-done = f32[512,2048]{1,0:T(8,128)} async-done(((f32[512,2048]{1,0:T(8,128)}), f32[512,2048]{1,0:T(8,128)}) %all-reduce.7.cloned.1.call-update) | async-done | bytes 4194320 | tf_op jit(solution)/shard_map/psum | solution.py:173
  281.8 8.3 fusion.76
  290.1 28.8 %all-gather.14.cloned.1.call-done = bf16[2048,1408]{1,0:T(8,128)(2,1)} async-done(((bf16[64,1408]{1,0:T(8,128)(2,1)}), bf16[2048,1408]{1,0:T(8,128)(2,1)}) %all-gather.14.cloned.1.call-update) | async-done | bytes 5767184 | tf_op jit(solution)/shard_map/all_gather | solution.py:188
  318.9 8.2 fusion.77
  327.1 23.8 %all-gather.22.cloned.1.call-done = bf16[512,2048]{1,0:T(8,128)(2,1)} async-done(((bf16[512,512]{1,0:T(8,128)(2,1)}), bf16[512,2048]{1,0:T(8,128)(2,1)}) %all-gather.22.cloned.1.call-update) | async-done | bytes 2097168 | tf_op jit(solution)/shard_map/all_gather | solution.py:126
  350.9 51.0 %all-gather.16.cloned.1.call-done = bf16[2048,1408]{1,0:T(8,128)(2,1)} async-done(((bf16[64,1408]{1,0:T(8,128)(2,1)}), bf16[2048,1408]{1,0:T(8,128)(2,1)}) %all-gather.16.cloned.1.call-update) | async-done | bytes 5767184 | tf_op jit(solution)/shard_map/all_gather | solution.py:189
  401.9 11.3 multiply_convert_fusion.3
  413.2 38.7 %all-gather.18.cloned.1.call-done = bf16[2048,1408]{1,0:T(8,128)(2,1)} async-done(((bf16[64,1408]{1,0:T(8,128)(2,1)}), bf16[2048,1408]{1,0:T(8,128)(2,1)}) %all-gather.18.cloned.1.call-update) | async-done | bytes 5767184 | tf_op jit(solution)/shard_map/all_gather | solution.py:200
  463.4 7.8 convolution_convert_fusion.5
  471.3 83.7 %all-reduce.9.cloned.1.call-done = f32[512,2048]{1,0:T(8,128)} async-done(((f32[512,2048]{1,0:T(8,128)}), f32[512,2048]{1,0:T(8,128)}) %all-reduce.9.cloned.1.call-update) | async-done | bytes 4194320 | tf_op jit(solution)/shard_map/psum | solution.py:213
  568.4 65.4 %while.33 = (s32[]{:T(128)}, f32[8,512,64]{1,2,0:T(8,128)}, f32[8,512,64]{1,2,0:T(8,128)}, f32[8,512,64]{1,2,0:T(8,128)}, bf16[8,512,64]{2,1,0:T(8,128)(2,1)}, /...) while((s32[]{:T(128)}, f32[8,512,64]{1,2,0:T(8,128)}, ...), condition=%wide.region_17.18_spmd.clone.clone, body=%wide.region_15.17_spmd.clone.sunk.clone | while | flops 170982912 | bytes 8994941 | solution.py:240
  656.6 8.0 convolution_convert_fusion.2
  664.7 8.1 convolution_convert_fusion.1
  673.1 7.9 convolution_convert_fusion
  685.4 7.3 all-to-all-start.3
  692.7 10.3 all-reduce.11.cloned.1.call-done
  710.1 7.3 all-to-all-start.5
  722.4 61.5 %reduce-scatter.13.cloned.1.call-done = bf16[64,64]{1,0:T(8,128)(2,1)} async-done(((bf16[2048,64]{1,0:T(8,128)(2,1)}), bf16[64,64]{1,0:T(8,128)(2,1)}) %reduce-scatter.13.cloned.1.call-update) | async-done | bytes 8208 | tf_op jit(solution)/shard_map/reduce_scatter | solution.py:277
  785.3 78.5 %reduce-scatter.15.cloned.1.call-done = bf16[64,64]{1,0:T(8,128)(2,1)} async-done(((bf16[2048,64]{1,0:T(8,128)(2,1)}), bf16[64,64]{1,0:T(8,128)(2,1)}) %reduce-scatter.15.cloned.1.call-update) | async-done | bytes 8208 | tf_op jit(solution)/shard_map/reduce_scatter | solution.py:280
  867.7 64.4 %all-reduce.2 = (bf16[2048]{0:T(1024)(128)(2,1)S(1)}, bf16[2048]{0:T(1024)(128)(2,1)S(1)}) all-reduce(bf16[2048]{0:T(1024)(128)(2,1)S(1)} %get-tuple-element.249, bf16[2048]{0:T(1024)(128)(2,1)S(1)} %copy-done.17), channel_id=5, replica_groups=mesh['row'=32,'col'=4] {'row'}, use_global_device_ids=true, to_apply=%region_23.24.clone | all-reduce | flops 4096 | bytes 16384
  935.4 10.1 reduce-scatter.11.cloned.1.call-done
  946.9 80.2 %reduce-scatter.17.cloned.1.call-done = bf16[64,512]{1,0:T(8,128)(2,1)} async-done(((bf16[2048,512]{1,0:T(8,128)(2,1)}), bf16[64,512]{1,0:T(8,128)(2,1)}) %reduce-scatter.17.cloned.1.call-update) | async-done | bytes 65552 | tf_op jit(solution)/shard_map/reduce_scatter | solution.py:283
  1028.6 86.8 %reduce-scatter.19.cloned.1.call-done = bf16[64,1408]{1,0:T(8,128)(2,1)} async-done(((bf16[2048,1408]{1,0:T(8,128)(2,1)}), bf16[64,1408]{1,0:T(8,128)(2,1)}) %reduce-scatter.19.cloned.1.call-update) | async-done | bytes 180240 | tf_op jit(solution)/shard_map/reduce_scatter | solution.py:218
  1117.1 87.1 %reduce-scatter.21.cloned.1.call-done = bf16[64,1408]{1,0:T(8,128)(2,1)} async-done(((bf16[2048,1408]{1,0:T(8,128)(2,1)}), bf16[64,1408]{1,0:T(8,128)(2,1)}) %reduce-scatter.21.cloned.1.call-update) | async-done | bytes 180240 | tf_op jit(solution)/shard_map/reduce_scatter | solution.py:221
  1205.8 86.6 %reduce-scatter.23.cloned.1.call-done = bf16[64,1408]{1,0:T(8,128)(2,1)} async-done(((bf16[2048,1408]{1,0:T(8,128)(2,1)}), bf16[64,1408]{1,0:T(8,128)(2,1)}) %reduce-scatter.23.cloned.1.call-update) | async-done | bytes 180240 | tf_op jit(solution)/shard_map/reduce_scatter | solution.py:224
  (293 shorter events, 257.4 us)
Async XLA Ops:
  12.3 38.3 %copy-start.14 = (s32[1024]{0:T(1024)}, s32[1024]{0:T(1024)S(1)}, u32[]{:S(2)}) copy-start(s32[1024]{0:T(1024)S(1)} %pad_clamp_fusion.3) | copy-start | bytes 12292
  16.6 15.7 %all-to-all-start.1 = ((s32[32,16,1]{1,2,0:T(1,128)}), s32[32,16,1]{1,2,0:T(1,128)S(1)}, u32[]{:S(2)}, u32[]{:S(2)}) async-start(s32[32,16,1]{1,2,0:T(1,128)} %bitcast.2), calls=%async_computation.1 | async-start | bytes 32768 | tf_op jit(solution)/shard_map/all_to_all | solution.py:121
  27.7 47.8 %copy-start.20 = (bf16[64,64]{1,0:T(8,128)(2,1)S(1)}, bf16[64,64]{1,0:T(8,128)(2,1)}, u32[]{:S(2)}) copy-start(bf16[64,64]{1,0:T(8,128)(2,1)} %param.24) | copy-start | bytes 24580
  32.3 15.7 %all-to-all-start = ((bf16[32,16,512]{2,1,0:T(8,128)(2,1)}), bf16[32,16,512]{2,1,0:T(8,128)(2,1)S(1)}, u32[]{:S(2)}, u32[]{:S(2)}) async-start(bf16[32,16,512]{2,1,0:T(8,128)(2,1)} %bitcast), calls=%async_computation | async-start | bytes 1048576 | tf_op jit(solution)/shard_map/all_to_all | solution.py:119
  36.2 66.3 %all-gather.20.cloned.1.call-start = ((), (), s32[]{:S(2)}) async-start(), calls=%async_computation.30 | async-start | bytes 2621440 | tf_op jit(solution)/shard_map/all_gather | solution.py:125
  48.0 56.8 %copy-start.21 = (f32[2048]{0:T(1024)S(1)}, f32[2048]{0:T(1024)}, u32[]{:S(2)}) copy-start(f32[2048]{0:T(1024)} %param.21) | copy-start | bytes 24580
  50.6 75.0 %all-gather.10.cloned.1.call-start = ((), (), s32[]{:S(2)}) async-start(), calls=%async_computation.14 | async-start | bytes 2162688 | tf_op jit(solution)/shard_map/all_gather | solution.py:129
  51.4 119.8 %all-gather.12.cloned.1.call-start = ((), (), s32[]{:S(2)}) async-start(), calls=%async_computation.15 | async-start | bytes 2162688 | tf_op jit(solution)/shard_map/all_gather | solution.py:132
  52.1 216.1 %all-reduce.7.cloned.1.call-start = ((), (), s32[]{:S(2)}) async-start(), calls=%async_computation.16 | async-start | bytes 8388608 | tf_op jit(solution)/shard_map/psum | solution.py:173
  52.2 55.3 %copy-start.26 = (f32[32]{0:T(128)}, f32[32]{0:T(128)S(1)}, u32[]{:S(2)}) copy-start(f32[32]{0:T(128)S(1)} %negate_power_fusion) | copy-start | bytes 388
  53.0 54.6 %copy-start.13 = (f32[512]{0:T(512)}, f32[512]{0:T(512)S(1)}, u32[]{:S(2)}) copy-start(f32[512]{0:T(512)S(1)} %fusion.70) | copy-start | bytes 6148
  75.5 34.8 %copy-start.8 = (bf16[2048,64]{1,0:T(8,128)(2,1)}, bf16[2048,64]{1,0:T(8,128)(2,1)S(1)}, u32[]{:S(2)}) copy-start(bf16[2048,64]{1,0:T(8,128)(2,1)S(1)} %all_gather.35) | copy-start | bytes 786436
  176.1 142.8 %all-gather.14.cloned.1.call-start = ((), (), s32[]{:S(2)}) async-start(), calls=%async_computation.17 | async-start | bytes 5947392 | tf_op jit(solution)/shard_map/all_gather | solution.py:188
  176.7 174.3 %all-gather.22.cloned.1.call-start = ((), (), s32[]{:S(2)}) async-start(), calls=%async_computation.31 | async-start | bytes 2621440 | tf_op jit(solution)/shard_map/all_gather | solution.py:126
  199.6 202.3 %all-gather.16.cloned.1.call-start = ((), (), s32[]{:S(2)}) async-start(), calls=%async_computation.18 | async-start | bytes 5947392 | tf_op jit(solution)/shard_map/all_gather | solution.py:189
  200.4 251.5 %all-gather.18.cloned.1.call-start = ((), (), s32[]{:S(2)}) async-start(), calls=%async_computation.20 | async-start | bytes 5947392 | tf_op jit(solution)/shard_map/all_gather | solution.py:200
  205.3 76.5 %all-to-all-start.2 = ((bf16[32,64,1408]{2,1,0:T(8,128)(2,1)}), bf16[32,64,1408]{2,1,0:T(8,128)(2,1)}, u32[]{:S(2)}, u32[]{:S(2)}) async-start(bf16[32,64,1408]{2,1,0:T(8,128)(2,1)} %stack.2), calls=%async_computation.2 | async-start | bytes 11534336 | tf_op jit(solution)/shard_map/all_to_all | solution.py:182
  210.2 62.8 %copy-start.12 = (f32[2048]{0:T(1024)S(1)}, f32[2048]{0:T(1024)}, u32[]{:S(2)}) copy-start(f32[2048]{0:T(1024)} %param.26) | copy-start | bytes 24580
  210.2 344.8 %all-reduce.9.cloned.1.call-start = ((), (), s32[]{:S(2)}) async-start(), calls=%async_computation.21 | async-start | bytes 8388608 | tf_op jit(solution)/shard_map/psum | solution.py:213
  463.1 218.0 %reduce-scatter.9.cloned.1.call-start = ((), (), s32[]{:S(2)}) async-start(), calls=%async_computation.19 | async-start | bytes 2621440 | tf_op jit(solution)/shard_map/reduce_scatter | solution.py:195
  471.2 231.7 %all-reduce.11.cloned.1.call-start = ((), (), s32[]{:S(2)}) async-start(), calls=%async_computation.22 | async-start | bytes 4194304 | tf_op jit(solution)/shard_map/psum | solution.py:269
  644.3 139.7 %reduce-scatter.13.cloned.1.call-start = ((), (), s32[]{:S(2)}) async-start(), calls=%async_computation.24 | async-start | bytes 540672 | tf_op jit(solution)/shard_map/reduce_scatter | solution.py:277
  646.2 217.6 %reduce-scatter.15.cloned.1.call-start = ((), (), s32[]{:S(2)}) async-start(), calls=%async_computation.25 | async-start | bytes 540672 | tf_op jit(solution)/shard_map/reduce_scatter | solution.py:280
  648.3 297.1 %reduce-scatter.11.cloned.1.call-start = ((), (), s32[]{:S(2)}) async-start(), calls=%async_computation.23 | async-start | bytes 2162688 | tf_op jit(solution)/shard_map/reduce_scatter | solution.py:274
  651.2 375.9 %reduce-scatter.17.cloned.1.call-start = ((), (), s32[]{:S(2)}) async-start(), calls=%async_computation.26 | async-start | bytes 2162688 | tf_op jit(solution)/shard_map/reduce_scatter | solution.py:283
  656.6 458.8 %reduce-scatter.19.cloned.1.call-start = ((), (), s32[]{:S(2)}) async-start(), calls=%async_computation.27 | async-start | bytes 5947392 | tf_op jit(solution)/shard_map/reduce_scatter | solution.py:218
  664.6 539.5 %reduce-scatter.21.cloned.1.call-start = ((), (), s32[]{:S(2)}) async-start(), calls=%async_computation.28 | async-start | bytes 5947392 | tf_op jit(solution)/shard_map/reduce_scatter | solution.py:221
  672.8 619.7 %reduce-scatter.23.cloned.1.call-start = ((), (), s32[]{:S(2)}) async-start(), calls=%async_computation.29 | async-start | bytes 5947392 | tf_op jit(solution)/shard_map/reduce_scatter | solution.py:224
  685.4 24.7 %all-to-all-start.3 = ((bf16[32,16,512]{2,1,0:T(8,128)(2,1)}), bf16[32,16,512]{2,1,0:T(8,128)(2,1)S(1)}, u32[]{:S(2)}, u32[]{:S(2)}) async-start(bf16[32,16,512]{2,1,0:T(8,128)(2,1)} %bitcast.195), calls=%async_computation.4 | async-start | bytes 1048576 | tf_op jit(solution)/shard_map/all_to_all | solution.py:291
  707.4 160.3 %copy-start.17 = (bf16[2048]{0:T(1024)(128)(2,1)S(1)}, bf16[2048]{0:T(1024)(128)(2,1)}, u32[]{:S(2)}) copy-start(bf16[2048]{0:T(1024)(128)(2,1)} %get-tuple-element.247) | copy-start | bytes 12292
  710.1 222.7 %all-to-all-start.5 = ((bf16[32,16,512]{2,1,0:T(8,128)(2,1)}), bf16[32,16,512]{2,1,0:T(8,128)(2,1)S(1)}, u32[]{:S(2)}, u32[]{:S(2)}) async-start(bf16[32,16,512]{2,1,0:T(8,128)(2,1)} %bitcast.25), calls=%async_computation.6 | async-start | bytes 1048576 | tf_op jit(solution)/shard_map/all_to_all | solution.py:292
  865.1 429.0 %copy-start.1 = (bf16[512,512]{1,0:T(8,128)(2,1)S(1)}, bf16[512,512]{1,0:T(8,128)(2,1)}, u32[]{:S(2)}) copy-start(bf16[512,512]{1,0:T(8,128)(2,1)} %param.17) | copy-start | bytes 1572868
  (21 other events, 156.9 us)
Sparse Core Ops, SparseCore 0:
  50.7 28.4 all-gather.19
  81.5 44.0 all-gather.9
  127.9 43.2 all-gather.11
  176.2 91.9 all-reduce.6
  270.6 48.3 all-gather.13
  321.1 29.7 all-gather.21
  353.4 48.4 all-gather.15
  404.4 47.4 all-gather.17
  463.2 91.7 all-reduce.8
  557.2 29.5 reduce-scatter.8
  644.4 58.5 all-reduce.10
  706.8 77.0 reduce-scatter.12
  787.4 76.3 reduce-scatter.14
  867.2 78.2 reduce-scatter.10
  948.8 78.2 reduce-scatter.16
  1030.7 84.6 reduce-scatter.18
  1119.5 84.6 reduce-scatter.20
  1207.8 84.6 reduce-scatter.22
